TPU v7x, 32 devices: a whole 2x2x4 slice. The times are simulated.
32 devices in a mesh: grp: 4 (over y, x), freq: 8 (over z, core).
Axes of the slice: x: 2, y: 2, z: 4, core: 2. Of those that a mesh axis runs over, the one named last changes fastest.
Arguments:
- transfer: bfloat16 [512, 2, 128, 512], P('freq', None, 'grp'), may hold values from -0.1875 to 0.1875
- adjoint: bfloat16 [512, 2, 512, 128], P('freq'), may hold values from -6 to 6
- lower_rows: bfloat16 [131072, 384], P(('grp', 'freq')), may hold values from -6 to 6
- pivot_store: bfloat16 [512, 384], P('grp'), may hold values from -0.3125 to 0.3125
- owners: int32 [3], replicated, may hold values from 0 to 3
- inverse_factor: bfloat16 [128, 128], replicated, as said below
Outputs:
- panel: bfloat16 [131072, 128], P(('grp', 'freq'))
Inputs may be any that keep to these rules, and one draw needn't show every extreme that they name: `inverse_factor`: upper triangular, with diagonal entries from 0.5 to 2.
All inputs are finite; a program needn't handle non-finite values.
Results may differ from a plain program's by a relative error of at most 0.0059.
Values may be sent and summed in bfloat16 or wider, within the bound.
A program may use at most 64 MiB of HBM per device.

v0:
```python
import math
import jax
import jax.numpy as jnp
from jax import lax
from jax.sharding import PartitionSpec as P

C = 128
NF = 512
PANELS = 3
NT = 1024


def make_table(samples, frequencies):
    time_steps = jnp.arange(samples, dtype=jnp.int32)[:, None]
    wave_numbers = jnp.arange(frequencies, dtype=jnp.int32)[None, :]
    phases = (time_steps * wave_numbers % samples).astype(jnp.float32) * (2.0 * math.pi / samples)
    factor = 1.0 / math.sqrt(frequencies)
    return jnp.stack([jnp.cos(phases) * factor, -jnp.sin(phases) * factor]).astype(jnp.bfloat16)


def product(left, right):
    return jnp.einsum("ksm,kmc->ksc", left, right, preferred_element_type=jnp.float32)


def per_device(transfer, adjoint, lower_rows, pivot_store, owners, inverse_factor):
    trans_real = transfer[:, 0]
    trans_imag = transfer[:, 1]
    adjoint_real = adjoint[:, 0]
    adjoint_imag = adjoint[:, 1]
    real_part = product(trans_real, adjoint_real) - product(trans_imag, adjoint_imag)
    imag_part = product(trans_real, adjoint_imag) + product(trans_imag, adjoint_real)
    spectra = jnp.stack([real_part, imag_part], axis=2).astype(jnp.bfloat16)
    table = make_table(NT, NF)
    hessian = jnp.einsum(
        "qtk,ksqc->stc",
        table,
        lax.all_to_all(spectra, "freq", split_axis=1, concat_axis=0, tiled=True),
        preferred_element_type=jnp.float32,
    )
    hessian = hessian.reshape(-1, hessian.shape[-1])
    owned_mask = (owners == lax.axis_index("grp")).astype(jnp.float32)
    local_blocks = pivot_store.reshape(C, PANELS, C).astype(jnp.float32) * owned_mask[None, :, None]
    combined = lax.psum(local_blocks.astype(jnp.bfloat16), "grp")
    pivots = combined.reshape(C, PANELS * C)
    update = lax.dot_general(
        lower_rows, pivots, (((1,), (1,)), ((), ())), preferred_element_type=jnp.float32
    )
    reduced = (hessian - update).astype(jnp.bfloat16)
    return jnp.dot(reduced, inverse_factor, preferred_element_type=jnp.float32).astype(jnp.bfloat16)


def solution(mesh):
    in_specs = (
        P("freq", None, "grp", None),
        P("freq", None, None, None),
        P(("grp", "freq"), None),
        P("grp", None),
        P(),
        P(),
    )
    out_specs = P(("grp", "freq"), None)
    return jax.shard_map(
        per_device, mesh=mesh, in_specs=in_specs, out_specs=out_specs, check_vma=False
    )
```

profile of v0, /device:TPU:0, one launch (start us, length us, event | category | flops | bytes accessed | tf_op | source)
XLA Modules:
  0.0 87.9 jit_solution(477097812663604727)
XLA Ops:
  6.5 5.5 %fusion.2 = f32[64,32,128]{2,1,0:T(8,128)S(1)} fusion(bf16[64,2,512,128]{3,2,1,0:T(8,128)(2,1)} %param.7, bf16[64,2,32,512]{3,2,1,0:T(8,128)(2,1)} %param.6), kind=kOutput, calls=%fused_computation.2 | convolution fusion | flops 268435456 | bytes 11534336 | tf_op jit(solution)/shard_map/ksm,kmc->ksc/dot_general | solution.py:22
  12.0 5.5 %fusion = f32[64,32,128]{2,1,0:T(8,128)S(1)} fusion(bf16[64,2,512,128]{3,2,1,0:T(8,128)(2,1)} %param.7, bf16[64,2,32,512]{3,2,1,0:T(8,128)(2,1)S(1)} %copy-done.6), kind=kOutput, calls=%fused_computation | convolution fusion | flops 268435456 | bytes 11534336 | tf_op jit(solution)/shard_map/ksm,kmc->ksc/dot_general | solution.py:22
  17.6 1.5 %copy-done.5 = bf16[64,2,512,128]{3,2,1,0:T(8,128)(2,1)S(1)} copy-done((bf16[64,2,512,128]{3,2,1,0:T(8,128)(2,1)S(1)}, bf16[64,2,512,128]{3,2,1,0:T(8,128)(2,1)}, u32[]{:S(2)}) %copy-start.5) | copy-done | bytes 16777240
  19.1 1.4 %fusion.52 = bf16[64,32,1,128]{3,1,0,2:T(8,128)(2,1)S(1)} fusion(f32[64,32,128]{2,1,0:T(8,128)S(1)} %fusion.2, bf16[64,2,512,128]{3,2,1,0:T(8,128)(2,1)S(1)} %copy-done.5, bf16[64,2,32,512]{3,2,1,0:T(8,128)(2,1)S(1)} %copy-done.6), kind=kOutput, calls=%fused_computation.44 | convolution fusion | flops 268959744 | bytes 12058624 | tf_op jit(solution)/shard_map/ksm,kmc->ksc/dot_general | solution.py:22
  20.5 1.4 %fusion.57 = bf16[64,32,1,128]{3,1,0,2:T(8,128)(2,1)S(1)} fusion(f32[64,32,128]{2,1,0:T(8,128)S(1)} %fusion, bf16[64,2,512,128]{3,2,1,0:T(8,128)(2,1)S(1)} %copy-done.5, bf16[64,2,32,512]{3,2,1,0:T(8,128)(2,1)S(1)} %copy-done.6), kind=kOutput, calls=%fused_computation.45 | convolution fusion | flops 268959744 | bytes 12058624 | tf_op jit(solution)/shard_map/ksm,kmc->ksc/dot_general | solution.py:22
  21.9 0.1 pad_maximum_fusion
  22.0 0.0 copy-start.3
  22.0 0.0 copy-start.7
  22.0 1.4 %copy.33 = bf16[64,32,2,128]{3,0,2,1:T(8,128)(2,1)} copy(bf16[64,32,2,128]{3,1,0,2:T(8,128)(2,1)S(1)} %pad_maximum_fusion) | data formatting | bytes 2097152 | tf_op jit(solution)/shard_map/stack | solution.py:32
  23.4 6.4 %all-to-all-start = ((bf16[64,32,2,128]{3,0,2,1:T(8,128)(2,1)}), bf16[64,32,2,128]{3,0,2,1:T(8,128)(2,1)}, u32[]{:S(2)}, u32[]{:S(2)}) async-start(bf16[64,32,2,128]{3,0,2,1:T(8,128)(2,1)} %copy.33), calls=%async_computation | async-start | bytes 2097152 | tf_op jit(solution)/shard_map/all_to_all | solution.py:37
  29.7 0.0 all-reduce.2.cloned.1.call-start
  29.8 0.1 copy.37
  29.9 0.7 fusion.62
  30.7 0.0 all-reduce.2.cloned.1.call-update
  30.7 9.3 %multiply_convert_fusion = (bf16[1,1024,512]{2,1,0:T(8,128)(2,1)}, bf16[1,1024,512]{2,1,0:T(8,128)(2,1)}) fusion(), kind=kLoop, calls=%fused_computation.30 | loop fusion | flops 9961472 | bytes 2097152 | tf_op jit(solution)/shard_map/convert.2
  40.0 16.4 %all-to-all-done = bf16[64,32,2,128]{3,0,2,1:T(8,128)(2,1)} async-done(((bf16[64,32,2,128]{3,0,2,1:T(8,128)(2,1)}), bf16[64,32,2,128]{3,0,2,1:T(8,128)(2,1)}, u32[]{:S(2)}, u32[]{:S(2)}) %all-to-all-start) | async-done | bytes 1048608 | tf_op jit(solution)/shard_map/all_to_all | solution.py:37
  56.4 1.4 %copy.34 = bf16[8,64,4,2,128]{4,1,0,3,2:T(8,128)(2,1)S(1)} copy(bf16[8,64,4,2,128]{4,1,3,2,0:T(8,128)(2,1)} %bitcast.7) | data formatting | bytes 2097152 | tf_op jit(solution)/shard_map/all_to_all | solution.py:37
  57.9 0.1 copy-done.1
  57.9 0.3 copy-done.2
  58.3 2.6 %fusion.31 = f32[4,1024,128]{1,2,0:T(8,128)} fusion(bf16[512,4,2,128]{3,0,2,1:T(8,128)(2,1)S(1)} %bitcast.87, bf16[1,1024,512]{2,1,0:T(8,128)(2,1)S(1)} %copy-done.1, bf16[1,1024,512]{2,1,0:T(8,128)(2,1)S(1)} %copy-done.2), kind=kOutput, calls=%fused_computation.39 | convolution fusion | flops 1074790400 | bytes 5242880 | tf_op jit(solution)/shard_map/qtk,ksqc->stc/dot_general | solution.py:34
  60.9 2.9 %copy.36 = f32[4,1024,128]{2,1,0:T(8,128)} copy(f32[4,1024,128]{1,2,0:T(8,128)} %fusion.31) | data formatting | bytes 4194304 | tf_op jit(solution)/shard_map/qtk,ksqc->stc/transpose | solution.py:34
  63.8 2.9 %copy.38 = f32[4096,128]{0,1:T(8,128)} copy(f32[4096,128]{1,0:T(8,128)} %bitcast.86) | data formatting | bytes 4194304 | tf_op jit(solution)/shard_map/reshape | solution.py:40
  66.7 10.3 %all-reduce.2.cloned.1.call-done = bf16[128,384]{0,1:T(8,128)(2,1)} async-done(((bf16[128,384]{0,1:T(8,128)(2,1)}), bf16[128,384]{0,1:T(8,128)(2,1)}) %all-reduce.2.cloned.1.call-update) | async-done | bytes 98320 | tf_op jit(solution)/shard_map/psum | solution.py:43
  77.0 4.1 %convolution_convert_fusion = bf16[4096,128]{1,0:T(8,128)(2,1)} fusion(bf16[128,128]{1,0:T(8,128)(2,1)S(1)} %copy-done.4, f32[4096,128]{0,1:T(8,128)} %copy.38, bf16[128,384]{0,1:T(8,128)(2,1)} %all-reduce.2.cloned.1.call-done, bf16[4096,384]{1,0:T(8,128)(2,1)S(1)} %copy-done), kind=kOutput, calls=%fused_computation.15 | convolution fusion | flops 538443776 | bytes 6422528 | tf_op jit(solution)/shard_map/dot_general | solution.py:49
  (12 shorter events, 0.0 us)
Async XLA Ops:
  6.5 70.5 %copy-start = (bf16[4096,384]{1,0:T(8,128)(2,1)S(1)}, bf16[4096,384]{1,0:T(8,128)(2,1)}, u32[]{:S(2)}) copy-start(bf16[4096,384]{1,0:T(8,128)(2,1)} %param.8) | copy-start | bytes 9437188
  6.5 5.5 %copy-start.6 = (bf16[64,2,32,512]{3,2,1,0:T(8,128)(2,1)S(1)}, bf16[64,2,32,512]{3,2,1,0:T(8,128)(2,1)}, u32[]{:S(2)}) copy-start(bf16[64,2,32,512]{3,2,1,0:T(8,128)(2,1)} %param.6) | copy-start | bytes 12582916
  6.5 12.6 %copy-start.5 = (bf16[64,2,512,128]{3,2,1,0:T(8,128)(2,1)S(1)}, bf16[64,2,512,128]{3,2,1,0:T(8,128)(2,1)}, u32[]{:S(2)}) copy-start(bf16[64,2,512,128]{3,2,1,0:T(8,128)(2,1)} %param.7) | copy-start | bytes 50331652
  22.0 7.8 %copy-start.3 = (bf16[128,384]{1,0:T(8,128)(2,1)S(1)}, bf16[128,384]{1,0:T(8,128)(2,1)}, u32[]{:S(2)}) copy-start(bf16[128,384]{1,0:T(8,128)(2,1)} %param.9) | copy-start | bytes 294916
  22.0 7.9 %copy-start.7 = (s32[3]{0:T(128)S(1)}, s32[3]{0:T(128)}, u32[]{:S(2)}) copy-start(s32[3]{0:T(128)} %param.10) | copy-start | bytes 40
  23.4 33.0 %all-to-all-start = ((bf16[64,32,2,128]{3,0,2,1:T(8,128)(2,1)}), bf16[64,32,2,128]{3,0,2,1:T(8,128)(2,1)}, u32[]{:S(2)}, u32[]{:S(2)}) async-start(bf16[64,32,2,128]{3,0,2,1:T(8,128)(2,1)} %copy.33), calls=%async_computation | async-start | bytes 2097152 | tf_op jit(solution)/shard_map/all_to_all | solution.py:37
  29.7 47.3 %all-reduce.2.cloned.1.call-start = ((), (), s32[]{:S(2)}) async-start(), calls=%async_computation.1 | async-start | bytes 196608 | tf_op jit(solution)/shard_map/psum | solution.py:43
  56.4 1.5 %copy-start.1 = (bf16[1,1024,512]{2,1,0:T(8,128)(2,1)S(1)}, bf16[1,1024,512]{2,1,0:T(8,128)(2,1)}, u32[]{:S(2)}) copy-start(bf16[1,1024,512]{2,1,0:T(8,128)(2,1)} %get-tuple-element.5) | copy-start | bytes 3145732
  56.4 1.9 %copy-start.2 = (bf16[1,1024,512]{2,1,0:T(8,128)(2,1)S(1)}, bf16[1,1024,512]{2,1,0:T(8,128)(2,1)}, u32[]{:S(2)}) copy-start(bf16[1,1024,512]{2,1,0:T(8,128)(2,1)} %get-tuple-element.6) | copy-start | bytes 3145732
  63.8 13.2 %copy-start.4 = (bf16[128,128]{1,0:T(8,128)(2,1)S(1)}, bf16[128,128]{1,0:T(8,128)(2,1)}, u32[]{:S(2)}) copy-start(bf16[128,128]{1,0:T(8,128)(2,1)} %param.11) | copy-start | bytes 98308
Sparse Core Ops, SparseCore 0:
  33.4 43.5 all-reduce.1
where the time goes:
time: 88.2 us; the launch traced here: 87.9 us
  waiting for transfers between devices  26.7 us (30%)
  matrix products  20.4 us (23%)
  between operations  13.5 us (15%)
  local copies, waits for them, and re-layouts  10.7 us (12%)
  other arithmetic  10.2 us (12%)
  starting transfers between devices  6.39 us (7%)
    all_to_all x1, waiting for transfers between devices, per_device(): lax.all_to_all(spectra, 'freq', split_axis=1, concat_axis=0, tiled=True)  16.4 us
    dot_general x4, matrix products, product(): jnp.einsum('ksm,kmc->ksc', left, right, preferred_element_type=jnp.float32)  13.8 us
    psum x1, waiting for transfers between devices, per_device(): combined = lax.psum(local_blocks.astype(jnp.bfloat16), 'grp')  10.3 us
    another operation x1, other arithmetic  9.32 us
    all_to_all x1, starting transfers between devices, per_device(): lax.all_to_all(spectra, 'freq', split_axis=1, concat_axis=0, tiled=True)  6.35 us
    dot_general x1, matrix products, per_device(): jnp.dot(reduced, inverse_factor, preferred_element_type=jnp.float32)  4.05 us
    transpose x1, local copies, waits for them, and re-layouts, per_device(): jnp.einsum('qtk,ksqc->stc', table, lax.all_to_all(spectra, 'freq', split_...  2.91 us
    reshape x1, local copies, waits for them, and re-layouts, per_device(): hessian = hessian.reshape(-1, hessian.shape[-1])  2.91 us
  transfers between devices with their start and end apart: 2, of which 2 were waited for; matrix products, arithmetic and copies ran while one was open for 23% of the time, Pallas kernels for 0%

commit v1 on v0

--- a/solution.py
+++ b/solution.py
@@ -40,7 +40,7 @@
     hessian = hessian.reshape(-1, hessian.shape[-1])
     owned_mask = (owners == lax.axis_index("grp")).astype(jnp.float32)
     local_blocks = pivot_store.reshape(C, PANELS, C).astype(jnp.float32) * owned_mask[None, :, None]
-    combined = lax.psum(local_blocks.astype(jnp.bfloat16), "grp")
+    combined = jnp.sum(lax.all_gather(local_blocks.astype(jnp.bfloat16), "grp"), axis=0)
     pivots = combined.reshape(C, PANELS * C)
     update = lax.dot_general(
         lower_rows, pivots, (((1,), (1,)), ((), ())), preferred_element_type=jnp.float32

time: 88.2 us -> 64.5 us (0.73)
  waiting for transfers between devices: 26.7 us -> 4.01 us
  between operations: 13.5 us -> 0.12 us
  blocking collectives: 0 us -> 10.6 us
  local copies, waits for them, and re-layouts: 10.7 us -> 12.5 us
    all_to_all x1, waiting for transfers between devices: 16.4 us -> 4.01 us  [per_device(): lax.all_to_all(spectra, 'freq', split_axis=1, concat_axis=0, tiled=True)]
    all_gather x0 -> x1, blocking collectives: none -> 10.6 us  [per_device(): lax.all_gather(local_blocks.astype(jnp.bfloat16), 'grp')]
    psum x1 -> x0, waiting for transfers between devices: 10.3 us -> none  [per_device(): combined = lax.psum(local_blocks.astype(jnp.bfloat16), 'grp')]
    reduce_sum x0 -> x1, local copies, waits for them, and re-layouts: none -> 1.01 us  [per_device(): jnp.sum(lax.all_gather(local_blocks.astype(jnp.bfloat16), 'grp'), axis=0)]
  transfers between devices with their start and end apart: 2 -> 1, of which waited for: 2 -> 1; matrix products, arithmetic and copies ran while one was open for 23% -> 19% of each run, Pallas kernels for 0% -> 0%
where the time goes in v1:
time: 64.5 us; the launch traced here: 64.2 us
  matrix products  20.3 us (31%)
  local copies, waits for them, and re-layouts  12.5 us (19%)
  blocking collectives  10.6 us (16%)
  other arithmetic  10.3 us (16%)
  starting transfers between devices  6.35 us (10%)
  waiting for transfers between devices  4.01 us (6%)
    dot_general x4, matrix products, product(): jnp.einsum('ksm,kmc->ksc', left, right, preferred_element_type=jnp.float32)  13.8 us
    all_gather x1, blocking collectives, per_device(): lax.all_gather(local_blocks.astype(jnp.bfloat16), 'grp')  10.6 us
    another operation x1, other arithmetic  9.36 us
    all_to_all x1, starting transfers between devices, per_device(): lax.all_to_all(spectra, 'freq', split_axis=1, concat_axis=0, tiled=True)  6.35 us
    all_to_all x1, waiting for transfers between devices, per_device(): lax.all_to_all(spectra, 'freq', split_axis=1, concat_axis=0, tiled=True)  4.01 us
    dot_general x1, matrix products, per_device(): jnp.dot(reduced, inverse_factor, preferred_element_type=jnp.float32)  3.99 us
    transpose x1, local copies, waits for them, and re-layouts, per_device(): jnp.einsum('qtk,ksqc->stc', table, lax.all_to_all(spectra, 'freq', split_...  2.93 us
    reshape x1, local copies, waits for them, and re-layouts, per_device(): hessian = hessian.reshape(-1, hessian.shape[-1])  2.9 us
  transfers between devices with their start and end apart: 1, of which 1 were waited for; matrix products, arithmetic and copies ran while one was open for 19% of the time, Pallas kernels for 0%

profile of v1, /device:TPU:0, one launch (start us, length us, event | category | flops | bytes accessed | tf_op | source)
XLA Modules:
  0.0 64.2 jit_solution(8504760456058720791)
XLA Ops:
  0.0 5.5 %fusion.2 = f32[64,32,128]{2,1,0:T(8,128)S(1)} fusion(bf16[64,2,512,128]{3,2,1,0:T(8,128)(2,1)} %param.7, bf16[64,2,32,512]{3,2,1,0:T(8,128)(2,1)} %param.6), kind=kOutput, calls=%fused_computation.2 | convolution fusion | flops 268435456 | bytes 11534336 | tf_op jit(solution)/shard_map/ksm,kmc->ksc/dot_general | solution.py:22
  5.5 5.5 %fusion = f32[64,32,128]{2,1,0:T(8,128)S(1)} fusion(bf16[64,2,512,128]{3,2,1,0:T(8,128)(2,1)} %param.7, bf16[64,2,32,512]{3,2,1,0:T(8,128)(2,1)S(1)} %copy-done.6), kind=kOutput, calls=%fused_computation | convolution fusion | flops 268435456 | bytes 11534336 | tf_op jit(solution)/shard_map/ksm,kmc->ksc/dot_general | solution.py:22
  11.1 1.5 %copy-done.5 = bf16[64,2,512,128]{3,2,1,0:T(8,128)(2,1)S(1)} copy-done((bf16[64,2,512,128]{3,2,1,0:T(8,128)(2,1)S(1)}, bf16[64,2,512,128]{3,2,1,0:T(8,128)(2,1)}, u32[]{:S(2)}) %copy-start.5) | copy-done | bytes 16777240
  12.6 1.4 %fusion.52 = bf16[64,32,1,128]{3,1,0,2:T(8,128)(2,1)S(1)} fusion(f32[64,32,128]{2,1,0:T(8,128)S(1)} %fusion.2, bf16[64,2,512,128]{3,2,1,0:T(8,128)(2,1)S(1)} %copy-done.5, bf16[64,2,32,512]{3,2,1,0:T(8,128)(2,1)S(1)} %copy-done.6), kind=kOutput, calls=%fused_computation.44 | convolution fusion | flops 268959744 | bytes 12058624 | tf_op jit(solution)/shard_map/ksm,kmc->ksc/dot_general | solution.py:22
  14.0 1.4 %fusion.57 = bf16[64,32,1,128]{3,1,0,2:T(8,128)(2,1)S(1)} fusion(f32[64,32,128]{2,1,0:T(8,128)S(1)} %fusion, bf16[64,2,512,128]{3,2,1,0:T(8,128)(2,1)S(1)} %copy-done.5, bf16[64,2,32,512]{3,2,1,0:T(8,128)(2,1)S(1)} %copy-done.6), kind=kOutput, calls=%fused_computation.45 | convolution fusion | flops 268959744 | bytes 12058624 | tf_op jit(solution)/shard_map/ksm,kmc->ksc/dot_general | solution.py:22
  15.3 0.1 pad_maximum_fusion
  15.4 0.0 copy-start.3
  15.5 1.4 %copy.45 = bf16[64,32,2,128]{3,0,2,1:T(8,128)(2,1)} copy(bf16[64,32,2,128]{3,1,0,2:T(8,128)(2,1)S(1)} %pad_maximum_fusion) | data formatting | bytes 2097152 | tf_op jit(solution)/shard_map/stack | solution.py:32
  16.9 6.4 %all-to-all-start = ((bf16[64,32,2,128]{3,0,2,1:T(8,128)(2,1)}), bf16[64,32,2,128]{3,0,2,1:T(8,128)(2,1)}, u32[]{:S(2)}, u32[]{:S(2)}) async-start(bf16[64,32,2,128]{3,0,2,1:T(8,128)(2,1)} %copy.45), calls=%async_computation | async-start | bytes 2097152 | tf_op jit(solution)/shard_map/all_to_all | solution.py:37
  23.2 0.1 copy.49
  23.4 0.1 fusion.62
  23.5 0.8 %copy.50 = bf16[1,128,3,128]{3,1,2,0:T(8,128)(2,1)} copy(bf16[1,128,3,128]{1,3,2,0:T(8,128)(2,1)S(1)} %fusion.62) | data formatting | bytes 196608 | tf_op jit(solution)/shard_map/convert_element_type | solution.py:43
  24.2 10.6 %all_gather.4 = bf16[4,128,3,128]{3,1,2,0:T(8,128)(2,1)S(1)} all-gather(bf16[1,128,3,128]{3,1,2,0:T(8,128)(2,1)} %copy.50), channel_id=1, replica_groups=mesh['grp'=4,'freq'=8] {'grp'}, dimensions={0}, use_global_device_ids=true | all-gather | bytes 491520 | tf_op jit(solution)/shard_map/all_gather | solution.py:43
  34.8 0.7 %reduce_sum.12 = bf16[128,3,128]{2,0,1:T(8,128)(2,1)} reduce(bf16[4,128,3,128]{3,1,2,0:T(8,128)(2,1)S(1)} %all_gather.4, bf16[]{:T(256)} %constant.26.clone.1), dimensions={0}, to_apply=%region_0.1 | reduce | flops 147456 | bytes 491522 | tf_op jit(solution)/shard_map/reduce_sum | solution.py:43
  35.5 1.0 %copy.51 = bf16[128,3,128]{0,2,1:T(8,128)(2,1)S(1)} copy(bf16[128,3,128]{2,0,1:T(8,128)(2,1)} %reduce_sum.12) | data formatting | bytes 196608 | tf_op jit(solution)/shard_map/reduce_sum | solution.py:43
  36.5 9.4 %multiply_convert_fusion = (bf16[1,1024,512]{2,1,0:T(8,128)(2,1)}, bf16[1,1024,512]{2,1,0:T(8,128)(2,1)}) fusion(), kind=kLoop, calls=%fused_computation.30 | loop fusion | flops 9961472 | bytes 2097152 | tf_op jit(solution)/shard_map/convert.3
  45.9 4.0 %all-to-all-done = bf16[64,32,2,128]{3,0,2,1:T(8,128)(2,1)} async-done(((bf16[64,32,2,128]{3,0,2,1:T(8,128)(2,1)}), bf16[64,32,2,128]{3,0,2,1:T(8,128)(2,1)}, u32[]{:S(2)}, u32[]{:S(2)}) %all-to-all-start) | async-done | bytes 1048608 | tf_op jit(solution)/shard_map/all_to_all | solution.py:37
  49.9 1.4 %copy.46 = bf16[8,64,4,2,128]{4,1,0,3,2:T(8,128)(2,1)S(1)} copy(bf16[8,64,4,2,128]{4,1,3,2,0:T(8,128)(2,1)} %bitcast.7) | data formatting | bytes 2097152 | tf_op jit(solution)/shard_map/all_to_all | solution.py:37
  51.3 0.1 copy-done.1
  51.4 0.3 copy-done.2
  51.7 2.6 %fusion.31 = f32[4,1024,128]{1,2,0:T(8,128)} fusion(bf16[512,4,2,128]{3,0,2,1:T(8,128)(2,1)S(1)} %bitcast.87, bf16[1,1024,512]{2,1,0:T(8,128)(2,1)S(1)} %copy-done.1, bf16[1,1024,512]{2,1,0:T(8,128)(2,1)S(1)} %copy-done.2), kind=kOutput, calls=%fused_computation.39 | convolution fusion | flops 1074790400 | bytes 5242880 | tf_op jit(solution)/shard_map/qtk,ksqc->stc/dot_general | solution.py:34
  54.3 2.9 %copy.48 = f32[4,1024,128]{2,1,0:T(8,128)} copy(f32[4,1024,128]{1,2,0:T(8,128)} %fusion.31) | data formatting | bytes 4194304 | tf_op jit(solution)/shard_map/qtk,ksqc->stc/transpose | solution.py:34
  57.3 2.9 %copy.52 = f32[4096,128]{0,1:T(8,128)} copy(f32[4096,128]{1,0:T(8,128)} %bitcast.86) | data formatting | bytes 4194304 | tf_op jit(solution)/shard_map/reshape | solution.py:40
  60.2 4.0 %convolution_convert_fusion = bf16[4096,128]{1,0:T(8,128)(2,1)} fusion(bf16[128,128]{1,0:T(8,128)(2,1)S(1)} %copy-done.4, f32[4096,128]{0,1:T(8,128)} %copy.52, bf16[128,384]{0,1:T(8,128)(2,1)S(1)} %bitcast.89, bf16[4096,384]{1,0:T(8,128)(2,1)S(1)} %copy-done), kind=kOutput, calls=%fused_computation.15 | convolution fusion | flops 538443776 | bytes 6422528 | tf_op jit(solution)/shard_map/dot_general | solution.py:49
  (13 shorter events, 0.0 us)
Async XLA Ops:
  0.0 60.2 %copy-start = (bf16[4096,384]{1,0:T(8,128)(2,1)S(1)}, bf16[4096,384]{1,0:T(8,128)(2,1)}, u32[]{:S(2)}) copy-start(bf16[4096,384]{1,0:T(8,128)(2,1)} %param.8) | copy-start | bytes 9437188
  0.0 5.5 %copy-start.6 = (bf16[64,2,32,512]{3,2,1,0:T(8,128)(2,1)S(1)}, bf16[64,2,32,512]{3,2,1,0:T(8,128)(2,1)}, u32[]{:S(2)}) copy-start(bf16[64,2,32,512]{3,2,1,0:T(8,128)(2,1)} %param.6) | copy-start | bytes 12582916
  0.0 12.6 %copy-start.5 = (bf16[64,2,512,128]{3,2,1,0:T(8,128)(2,1)S(1)}, bf16[64,2,512,128]{3,2,1,0:T(8,128)(2,1)}, u32[]{:S(2)}) copy-start(bf16[64,2,512,128]{3,2,1,0:T(8,128)(2,1)} %param.7) | copy-start | bytes 50331652
  15.4 7.8 %copy-start.3 = (bf16[128,384]{1,0:T(8,128)(2,1)S(1)}, bf16[128,384]{1,0:T(8,128)(2,1)}, u32[]{:S(2)}) copy-start(bf16[128,384]{1,0:T(8,128)(2,1)} %param.9) | copy-start | bytes 294916
  15.5 7.9 %copy-start.7 = (s32[3]{0:T(128)S(1)}, s32[3]{0:T(128)}, u32[]{:S(2)}) copy-start(s32[3]{0:T(128)} %param.10) | copy-start | bytes 40
  16.9 33.0 %all-to-all-start = ((bf16[64,32,2,128]{3,0,2,1:T(8,128)(2,1)}), bf16[64,32,2,128]{3,0,2,1:T(8,128)(2,1)}, u32[]{:S(2)}, u32[]{:S(2)}) async-start(bf16[64,32,2,128]{3,0,2,1:T(8,128)(2,1)} %copy.45), calls=%async_computation | async-start | bytes 2097152 | tf_op jit(solution)/shard_map/all_to_all | solution.py:37
  49.9 1.5 %copy-start.1 = (bf16[1,1024,512]{2,1,0:T(8,128)(2,1)S(1)}, bf16[1,1024,512]{2,1,0:T(8,128)(2,1)}, u32[]{:S(2)}) copy-start(bf16[1,1024,512]{2,1,0:T(8,128)(2,1)} %get-tuple-element.5) | copy-start | bytes 3145732
  49.9 1.9 %copy-start.2 = (bf16[1,1024,512]{2,1,0:T(8,128)(2,1)S(1)}, bf16[1,1024,512]{2,1,0:T(8,128)(2,1)}, u32[]{:S(2)}) copy-start(bf16[1,1024,512]{2,1,0:T(8,128)(2,1)} %get-tuple-element.6) | copy-start | bytes 3145732
  57.3 2.9 %copy-start.4 = (bf16[128,128]{1,0:T(8,128)(2,1)S(1)}, bf16[128,128]{1,0:T(8,128)(2,1)}, u32[]{:S(2)}) copy-start(bf16[128,128]{1,0:T(8,128)(2,1)} %param.11) | copy-start | bytes 98308
